TPU v7x, 256 devices: a whole 4x4x8 slice. The times are simulated.
256 devices in a mesh: section: 8 (over z), dp: 32 (over x, y, core).
Axes of the slice: x: 4, y: 4, z: 8, core: 2. Of those that a mesh axis runs over, the one named last changes fastest.
Arguments:
- tokens: bfloat16 [4096, 5120], P('dp'), may hold values from -6 to 6
- cotangent: bfloat16 [4096, 5120], P('dp'), may hold values from -0.75 to 0.75
- section_layers: int32 [8], P('section'), may hold values from 1 to 2, as said below
- up_rows: int32 [16, 112], P('section'), may hold values from 0 to 39, as said below
- down_cols: int32 [16, 112], P('section'), may hold values from 0 to 39, as said below
- up_blocks: bfloat16 [16, 112, 128, 128], P('section', None, 'dp'), may hold values from -0.5 to 0.5
- down_blocks: bfloat16 [16, 112, 128, 128], P('section', None, 'dp'), may hold values from -0.3125 to 0.3125
Outputs:
- section_outputs: bfloat16 [8, 4096, 5120], P('section', 'dp')
- section_input_grads: bfloat16 [8, 4096, 5120], P('section', 'dp')
- up_grads: bfloat16 [16, 112, 128, 128], P('section', None, 'dp')
- down_grads: bfloat16 [16, 112, 128, 128], P('section', None, 'dp')
Inputs may be any that keep to these rules, and one draw needn't show every extreme that they name: `section_layers`: each section applies one or two layers; in every draw some section applies two and some section applies one. `up_rows`: in each layer every feature block is read by 2 or 3 hidden blocks. `down_cols`: in each layer every feature block is written by 2 or 3 hidden blocks.
All inputs are finite; a program needn't handle non-finite values.
Results may differ from a plain program's by a relative error of at most 0.029.
Values may be sent and summed in bfloat16 or wider, within the bound.
No kernel may reach another device: no remote copies, remote signals or barrier semaphores. Data moves between devices by JAX's collectives and lax.ppermute only.
A program may use at most 192 MiB of HBM per device.

v0:
```python
import jax
import jax.numpy as jnp
from jax import lax
from jax.sharding import PartitionSpec as P

MICRO = 2


root_coef = 0.7978845608028654
cubic_coef = 0.044715


def passed_along(value, axis, steps):
    count = lax.axis_size(axis)
    first, last = (max(0, -steps), min(count, count - steps))
    return lax.ppermute(value, axis, [(source, source + steps) for source in range(first, last)])


def gelu_parts(inputs):
    inner = root_coef * (inputs + cubic_coef * inputs * inputs * inputs)
    tangent = jnp.tanh(inner)
    values = 0.5 * inputs * (1.0 + tangent)
    slope = 0.5 * (1.0 + tangent) + 0.5 * inputs * (1.0 - tangent * tangent) * root_coef * (
        1.0 + 3.0 * cubic_coef * inputs * inputs
    )
    return (values, slope)


def slot_table(ids, count, slot_count):
    hidden_count = ids.shape[0]
    feature_range = jnp.arange(count, dtype=jnp.int32)
    member = (ids[:, None] == feature_range[None, :]).astype(jnp.int32)
    order_rank = jnp.sum((jnp.cumsum(member, axis=0) - member) * member, axis=1)
    matches = (ids[None, None, :] == feature_range[:, None, None]) & (
        order_rank[None, None, :] == jnp.arange(slot_count, dtype=jnp.int32)[None, :, None]
    )
    has_block = jnp.any(matches, axis=2)
    block_index = jnp.sum(
        matches.astype(jnp.int32) * jnp.arange(hidden_count, dtype=jnp.int32)[None, None, :], axis=2
    )
    return jnp.where(has_block, block_index, hidden_count)


def pad_blocks(values, axis):
    shape = list(values.shape)
    shape[axis] = 1
    return jnp.concatenate([values, jnp.zeros(shape, values.dtype)], axis=axis)


def arrange(w_up, w_down, row_ids, col_ids, count):
    hidden_count, block = (w_up.shape[0], w_up.shape[1])
    slot_count = hidden_count // count + 1
    down_table = slot_table(col_ids, count, slot_count).reshape(-1)
    up_table = slot_table(row_ids, count, slot_count).reshape(-1)
    down_sorted = jnp.take(pad_blocks(w_down, 0), down_table, axis=0).reshape(
        count, slot_count * block, block
    )
    up_sorted = jnp.take(pad_blocks(w_up, 0), up_table, axis=0).reshape(
        count, slot_count, block, block
    )
    return (w_up, w_down, row_ids, col_ids, down_table, up_table, down_sorted, up_sorted)


def layer_parts(hidden, params):
    w_up = params[0]
    row_ids = params[2]
    count_rows, width = hidden.shape
    block = w_up.shape[2]
    hidden_f = hidden.astype(jnp.float32)
    inv_rms = lax.rsqrt(jnp.mean(hidden_f * hidden_f, axis=-1, keepdims=True) + 1e-05)
    normal = hidden_f * inv_rms
    normed = normal.astype(jnp.bfloat16)
    picked = jnp.take(normed.reshape(count_rows, width // block, block), row_ids, axis=1)
    pre_act = jnp.einsum("rfi,fio->rfo", picked, w_up, preferred_element_type=jnp.float32)
    return (hidden_f, inv_rms, normal, picked, pre_act)


def layer_forward(hidden, params):
    down_table, down_sorted = (params[4], params[6])
    count_rows, width = hidden.shape
    count = down_sorted.shape[0]
    hidden_f, inv_rms, normal, picked, pre_act = layer_parts(hidden, params)
    values, slope = gelu_parts(pre_act)
    gated = values.astype(jnp.bfloat16)
    grouped = jnp.take(pad_blocks(gated, 1), down_table, axis=1).reshape(
        count_rows, count, down_sorted.shape[1]
    )
    summed = jnp.einsum("rkj,kjo->rko", grouped, down_sorted, preferred_element_type=jnp.float32)
    return (hidden_f + summed.reshape(count_rows, width)).astype(jnp.bfloat16)


def pre_gradient(hidden, cot, params):
    w_down, col_ids = (params[1], params[3])
    count_rows, width = hidden.shape
    block = w_down.shape[2]
    hidden_f, inv_rms, normal, picked, pre_act = layer_parts(hidden, params)
    values, slope = gelu_parts(pre_act)
    cot_picked = jnp.take(cot.reshape(count_rows, width // block, block), col_ids, axis=1)
    d_gated = jnp.einsum("rfo,fio->rfi", cot_picked, w_down, preferred_element_type=jnp.float32)
    d_pre = (d_gated * slope).astype(jnp.bfloat16)
    return (inv_rms, normal, picked, values.astype(jnp.bfloat16), cot_picked, d_pre)


def layer_backward(hidden, cot, params):
    up_table, up_sorted = (params[5], params[7])
    count_rows, width = hidden.shape
    count, slot_count, block = (up_sorted.shape[0], up_sorted.shape[1], up_sorted.shape[2])
    inv_rms, normal, picked, gated, cot_picked, d_pre = pre_gradient(hidden, cot, params)
    grouped = jnp.take(pad_blocks(d_pre, 1), up_table, axis=1).reshape(
        count_rows, count, slot_count, block
    )
    d_normal = jnp.einsum(
        "rkso,ksio->rki", grouped, up_sorted, preferred_element_type=jnp.float32
    ).reshape(count_rows, width)
    d_hidden = cot.astype(jnp.float32) + inv_rms * (
        d_normal - normal * jnp.mean(d_normal * normal, axis=-1, keepdims=True)
    )
    return d_hidden.astype(jnp.bfloat16)


def block_grads(hidden, cot, params):
    inv_rms, normal, picked, gated, cot_picked, d_pre = pre_gradient(hidden, cot, params)
    grad_up = jnp.einsum("rfi,rfo->fio", picked, d_pre, preferred_element_type=jnp.float32)
    grad_down = jnp.einsum("rfi,rfo->fio", gated, cot_picked, preferred_element_type=jnp.float32)
    return (grad_up, grad_down)


def put(buffer, value, slot_idx, is_live):
    older = lax.dynamic_index_in_dim(buffer, slot_idx, 0, keepdims=False)
    return lax.dynamic_update_index_in_dim(buffer, jnp.where(is_live, value, older), slot_idx, 0)


def local(tokens, cotangent, section_layers, up_rows, down_cols, up_blocks, down_blocks):
    section_idx = lax.axis_index("section")
    last_section = lax.axis_size("section") - 1
    layer_count = section_layers[0]
    up_full, down_full = (
        lax.all_gather(up_blocks, "dp", axis=2, tiled=True),
        lax.all_gather(down_blocks, "dp", axis=2, tiled=True),
    )
    tok_rows, width = tokens.shape
    block = up_full.shape[2]
    groups = MICRO

    def send_ahead(values):
        return passed_along(values, "section", 1)

    def send_back(values):
        return passed_along(values, "section", -1)

    group_rows = tok_rows // groups
    first_params = arrange(up_full[0], down_full[0], up_rows[0], down_cols[0], width // block)
    second_params = arrange(up_full[1], down_full[1], up_rows[1], down_cols[1], width // block)
    tok_groups = tokens.reshape(groups, group_rows, width)
    cot_groups = cotangent.reshape(groups, group_rows, width)
    ticks = groups + last_section

    def section_forward(values):
        after_one = layer_forward(values, first_params)
        result = lax.cond(
            layer_count > 1,
            lambda inner: layer_forward(inner, second_params),
            lambda inner: inner,
            after_one,
        )
        return (after_one, result)

    def blank_forward(values):
        return (jnp.zeros_like(values), jnp.zeros_like(values))

    def forward_tick(tick_now, carry):
        incoming, kept_in, kept_mid, kept_out = carry
        micro_idx = tick_now - section_idx
        is_live = (micro_idx >= 0) & (micro_idx < groups)
        slot_idx = jnp.clip(micro_idx, 0, groups - 1)
        source = jnp.where(
            section_idx == 0,
            lax.dynamic_index_in_dim(tok_groups, slot_idx, 0, keepdims=False),
            incoming,
        )
        middle, result = lax.cond(is_live, section_forward, blank_forward, source)
        kept_in = put(kept_in, source, slot_idx, is_live)
        kept_mid = put(kept_mid, middle, slot_idx, is_live)
        kept_out = put(kept_out, result, slot_idx, is_live)
        return (send_ahead(result), kept_in, kept_mid, kept_out)

    zero_rows = jnp.zeros((group_rows, width), jnp.bfloat16)
    zero_acts = jnp.zeros((groups, group_rows, width), jnp.bfloat16)
    unused, kept_in, kept_mid, kept_out = lax.fori_loop(
        0, ticks, forward_tick, (zero_rows, zero_acts, zero_acts, zero_acts)
    )

    def section_backward(triple):
        section_input, middle, cot = triple
        cot_mid = lax.cond(
            layer_count > 1,
            lambda inner: layer_backward(inner[0], inner[1], second_params),
            lambda inner: inner[1],
            (middle, cot),
        )
        d_input = layer_backward(section_input, cot_mid, first_params)
        return (d_input, cot_mid)

    def blank_backward(triple):
        return (jnp.zeros_like(triple[2]), jnp.zeros_like(triple[2]))

    def backward_tick(tick_now, carry):
        incoming, kept_dx, kept_top, kept_inner = carry
        micro_idx = tick_now - (last_section - section_idx)
        is_live = (micro_idx >= 0) & (micro_idx < groups)
        slot_idx = jnp.clip(micro_idx, 0, groups - 1)
        source = jnp.where(
            section_idx == last_section,
            lax.dynamic_index_in_dim(cot_groups, slot_idx, 0, keepdims=False),
            incoming,
        )
        section_input = lax.dynamic_index_in_dim(kept_in, slot_idx, 0, keepdims=False)
        middle = lax.dynamic_index_in_dim(kept_mid, slot_idx, 0, keepdims=False)
        d_input, cot_mid = lax.cond(
            is_live, section_backward, blank_backward, (section_input, middle, source)
        )
        kept_dx = put(kept_dx, d_input, slot_idx, is_live)
        kept_top = put(kept_top, source, slot_idx, is_live)
        kept_inner = put(kept_inner, cot_mid, slot_idx, is_live)
        return (send_back(d_input), kept_dx, kept_top, kept_inner)

    carry = lax.fori_loop(0, ticks, backward_tick, (zero_rows, zero_acts, zero_acts, zero_acts))
    unused, kept_dx, kept_top, kept_inner = carry
    up_one, down_one = block_grads(
        kept_in.reshape(tok_rows, width), kept_inner.reshape(tok_rows, width), first_params
    )
    up_two, down_two = block_grads(
        kept_mid.reshape(tok_rows, width), kept_top.reshape(tok_rows, width), second_params
    )
    active = layer_count > 1
    up_two = jnp.where(active, up_two, 0.0)
    down_two = jnp.where(active, down_two, 0.0)
    summed_up, summed_down = (
        lax.psum_scatter(
            jnp.stack([up_one, up_two]).astype(jnp.bfloat16), "dp", scatter_dimension=2, tiled=True
        ).astype(jnp.float32),
        lax.psum_scatter(
            jnp.stack([down_one, down_two]).astype(jnp.bfloat16),
            "dp",
            scatter_dimension=2,
            tiled=True,
        ).astype(jnp.float32),
    )
    return (
        kept_out.reshape(1, tok_rows, width),
        kept_dx.reshape(1, tok_rows, width),
        summed_up.astype(jnp.bfloat16),
        summed_down.astype(jnp.bfloat16),
    )


def solution(mesh):
    in_specs = (
        P("dp", None),
        P("dp", None),
        P("section"),
        P("section", None),
        P("section", None),
        P("section", None, "dp", None),
        P("section", None, "dp", None),
    )
    out_specs = (
        P("section", "dp", None),
        P("section", "dp", None),
        P("section", None, "dp", None),
        P("section", None, "dp", None),
    )
    return jax.shard_map(local, mesh=mesh, in_specs=in_specs, out_specs=out_specs, check_vma=False)
```

profile of v0, /device:TPU:1, one launch (start us, length us, event | category | flops | bytes accessed | tf_op | source)
XLA Modules:
  0.0 1572.2 jit_solution(11359778735014715467)
XLA Ops:
  22.7 48.4 %all-gather.3.cloned.1.call-done = bf16[2,112,128,128]{3,1,0,2:T(8,128)(2,1)} async-done(((bf16[2,112,4,128]{3,1,0,2:T(8,128)(2,1)}), bf16[2,112,128,128]{3,1,0,2:T(8,128)(2,1)}) %all-gather.3.cloned.1.call-update) | async-done | bytes 7340048 | tf_op jit(solution)/shard_map/all_gather | solution.py:138
  71.1 4.4 fusion.201
  78.6 5.2 copy_bitcast_fusion.5
  83.8 45.4 %all-gather.5.cloned.1.call-done = bf16[2,112,128,128]{3,1,0,2:T(8,128)(2,1)} async-done(((bf16[2,112,4,128]{3,1,0,2:T(8,128)(2,1)}), bf16[2,112,128,128]{3,1,0,2:T(8,128)(2,1)}) %all-gather.5.cloned.1.call-update) | async-done | bytes 7340048 | tf_op jit(solution)/shard_map/all_gather | solution.py:139
  129.2 4.4 fusion.200
  141.7 5.1 gather_fusion.10
  146.8 4.6 broadcast_select_fusion.5
  153.5 5.0 gather_fusion.11
  158.5 4.5 broadcast_select_fusion.4
  172.1 373.9 %while.41 = (s32[]{:T(128)}, bf16[64,5120]{1,0:T(8,128)(2,1)S(1)}, bf16[2,64,5120]{2,1,0:T(8,128)(2,1)}, bf16[2,64,5120]{2,1,0:T(8,128)(2,1)}, bf16[2,64,5120]{2...) while((s32[]{:T(128)}, bf16[64,5120]{1,0:T(8,128)(2,1)S(1)}, ...), condition=%wide.region_15.19_spmd, body=%wide.region_8.18_spmd.sunk | while | flops 1000612096 | bytes 98235312 | solution.py:189
  175.8 37.7 %conditional.6 = (bf16[64,5120]{1,0:T(8,128)(2,1)}, bf16[64,5120]{1,0:T(8,128)(2,1)}) conditional(s32[]{:T(128)} %convert_element_type.321, () %tuple.148, (bf16[64,5120]{1,0:T(8,128)(2,1)S(1)}, s32[112]{0:T(128)S(1)}, bf16[112,128,128]{2,1,0:T(8,128)(2,1)}, s32[120]{0:T(128)S(1)}, bf16[40,384,128]{2,1,0:T(8,128)(2,1)}, /*index=5*/s32[]{:T(128)}, ...), branch_computations={%region_9.10_spmd, %region_10.17_spmd} | conditional | flops 999301376 | bytes 84471856 | solution.py:181
  193.3 20.2 %conditional = (bf16[64,5120]{1,0:T(8,128)(2,1)}) conditional(s32[]{:T(128)} %convert_element_type.149, bf16[64,5120]{1,0:T(8,128)(2,1)} %fusion.34, (bf16[64,5120]{1,0:T(8,128)(2,1)}, s32[112]{0:T(128)S(1)}, bf16[112,128,128]{2,1,0:T(8,128)(2,1)}, s32[120]{0:T(128)S(1)}, bf16[40,384,128]{2,1,0:T(8,128)(2,1)}) %tuple.73), branch_computations={%region_12.14_spmd, %region_13.16_spmd} | conditional | flops 499650688 | bytes 42235896 | solution.py:160
  219.8 9.4 collective-permute-done
  232.5 37.7 %conditional.6 = (bf16[64,5120]{1,0:T(8,128)(2,1)}, bf16[64,5120]{1,0:T(8,128)(2,1)}) conditional(s32[]{:T(128)} %convert_element_type.321, () %tuple.148, (bf16[64,5120]{1,0:T(8,128)(2,1)S(1)}, s32[112]{0:T(128)S(1)}, bf16[112,128,128]{2,1,0:T(8,128)(2,1)}, s32[120]{0:T(128)S(1)}, bf16[40,384,128]{2,1,0:T(8,128)(2,1)}, /*index=5*/s32[]{:T(128)}, ...), branch_computations={%region_9.10_spmd, %region_10.17_spmd} | conditional | flops 999301376 | bytes 84471856 | solution.py:181
  250.1 20.2 %conditional = (bf16[64,5120]{1,0:T(8,128)(2,1)}) conditional(s32[]{:T(128)} %convert_element_type.149, bf16[64,5120]{1,0:T(8,128)(2,1)} %fusion.34, (bf16[64,5120]{1,0:T(8,128)(2,1)}, s32[112]{0:T(128)S(1)}, bf16[112,128,128]{2,1,0:T(8,128)(2,1)}, s32[120]{0:T(128)S(1)}, bf16[40,384,128]{2,1,0:T(8,128)(2,1)}) %tuple.73), branch_computations={%region_12.14_spmd, %region_13.16_spmd} | conditional | flops 499650688 | bytes 42235896 | solution.py:160
  279.3 8.5 collective-permute-done
  293.0 40.0 %collective-permute-start = (bf16[64,5120]{1,0:T(8,128)(2,1)}, bf16[64,5120]{1,0:T(8,128)(2,1)S(1)}, u32[]{:S(2)}, u32[]{:S(2)}) collective-permute-start(bf16[64,5120]{1,0:T(8,128)(2,1)} %get-tuple-element.1449), channel_id=1, source_target_pairs={{0,32},{32,64},{64,96},{96,128},{128,160},{160,192},{192,224},{1,3... | collective-permute-start | bytes 1966088 | tf_op jit(solution)/shard_map/while/body/eval_jaxpr/ppermute | solution.py:16
  336.6 9.0 collective-permute-done
  358.4 8.1 collective-permute-done
  371.7 20.2 %collective-permute-start = (bf16[64,5120]{1,0:T(8,128)(2,1)}, bf16[64,5120]{1,0:T(8,128)(2,1)S(1)}, u32[]{:S(2)}, u32[]{:S(2)}) collective-permute-start(bf16[64,5120]{1,0:T(8,128)(2,1)} %get-tuple-element.1449), channel_id=1, source_target_pairs={{0,32},{32,64},{64,96},{96,128},{128,160},{160,192},{192,224},{1,3... | collective-permute-start | bytes 1966088 | tf_op jit(solution)/shard_map/while/body/eval_jaxpr/ppermute | solution.py:16
  395.6 7.5 collective-permute-done
  416.0 6.7 collective-permute-done
  427.7 20.5 %collective-permute-start = (bf16[64,5120]{1,0:T(8,128)(2,1)}, bf16[64,5120]{1,0:T(8,128)(2,1)S(1)}, u32[]{:S(2)}, u32[]{:S(2)}) collective-permute-start(bf16[64,5120]{1,0:T(8,128)(2,1)} %get-tuple-element.1449), channel_id=1, source_target_pairs={{0,32},{32,64},{64,96},{96,128},{128,160},{160,192},{192,224},{1,3... | collective-permute-start | bytes 1966088 | tf_op jit(solution)/shard_map/while/body/eval_jaxpr/ppermute | solution.py:16
  452.0 6.1 collective-permute-done
  463.2 4.9 collective-permute-start
  471.8 5.5 collective-permute-done
  482.5 41.2 %collective-permute-start = (bf16[64,5120]{1,0:T(8,128)(2,1)}, bf16[64,5120]{1,0:T(8,128)(2,1)S(1)}, u32[]{:S(2)}, u32[]{:S(2)}) collective-permute-start(bf16[64,5120]{1,0:T(8,128)(2,1)} %get-tuple-element.1449), channel_id=1, source_target_pairs={{0,32},{32,64},{64,96},{96,128},{128,160},{160,192},{192,224},{1,3... | collective-permute-start | bytes 1966088 | tf_op jit(solution)/shard_map/while/body/eval_jaxpr/ppermute | solution.py:16
  527.3 4.7 collective-permute-done
  553.6 5.2 gather_fusion.12
  558.8 4.5 broadcast_select_fusion.3
  563.3 5.2 gather_fusion.13
  568.5 4.5 broadcast_select_fusion.2
  575.6 711.1 %while.42 = (s32[]{:T(128)}, bf16[64,5120]{1,0:T(8,128)(2,1)S(1)}, bf16[2,64,5120]{2,1,0:T(8,128)(2,1)}, bf16[2,64,5120]{2,1,0:T(8,128)(2,1)S(1)}, bf16[2,64,512...) while((s32[]{:T(128)}, bf16[64,5120]{1,0:T(8,128)(2,1)S(1)}, ...), condition=%wide.region_33.37_spmd, body=%wide.region_24.36_spmd.sunk | while | flops 1495805952 | bytes 174535680 | solution.py:227
  583.3 8.2 collective-permute-done.1
  599.3 23.1 %collective-permute-done.1 = bf16[64,5120]{1,0:T(8,128)(2,1)S(1)} collective-permute-done((bf16[64,5120]{1,0:T(8,128)(2,1)S(1)}, bf16[64,5120]{1,0:T(8,128)(2,1)S(1)}, u32[]{:S(2)}, u32[]{:S(2)}) %collective-permute-start.1) | collective-permute-done | bytes 655392 | tf_op jit(solution)/shard_map/while/body/eval_jaxpr/ppermute | solution.py:16
  630.1 8.2 collective-permute-done.1
  646.0 40.7 %collective-permute-done.1 = bf16[64,5120]{1,0:T(8,128)(2,1)S(1)} collective-permute-done((bf16[64,5120]{1,0:T(8,128)(2,1)S(1)}, bf16[64,5120]{1,0:T(8,128)(2,1)S(1)}, u32[]{:S(2)}, u32[]{:S(2)}) %collective-permute-start.1) | collective-permute-done | bytes 655392 | tf_op jit(solution)/shard_map/while/body/eval_jaxpr/ppermute | solution.py:16
  694.5 8.1 collective-permute-done.1
  710.3 41.1 %collective-permute-done.1 = bf16[64,5120]{1,0:T(8,128)(2,1)S(1)} collective-permute-done((bf16[64,5120]{1,0:T(8,128)(2,1)S(1)}, bf16[64,5120]{1,0:T(8,128)(2,1)S(1)}, u32[]{:S(2)}, u32[]{:S(2)}) %collective-permute-start.1) | collective-permute-done | bytes 655392 | tf_op jit(solution)/shard_map/while/body/eval_jaxpr/ppermute | solution.py:16
  759.1 367.8 %collective-permute-done.1 = bf16[64,5120]{1,0:T(8,128)(2,1)S(1)} collective-permute-done((bf16[64,5120]{1,0:T(8,128)(2,1)S(1)}, bf16[64,5120]{1,0:T(8,128)(2,1)S(1)}, u32[]{:S(2)}, u32[]{:S(2)}) %collective-permute-start.1) | collective-permute-done | bytes 655392 | tf_op jit(solution)/shard_map/while/body/eval_jaxpr/ppermute | solution.py:16
  1129.5 65.7 %conditional.7 = (bf16[64,5120]{1,0:T(8,128)(2,1)S(1)}, bf16[64,5120]{1,0:T(8,128)(2,1)S(1)}) conditional(s32[]{:T(128)} %convert_element_type.322, () %tuple.153, (s32[]{:T(128)}, bf16[64,5120]{1,0:T(8,128)(2,1)S(1)}, bf16[2,64,5120]{2,1,0:T(8,128)(2,1)}, s32[]{:T(128)}, s32[112]{0:T(128)S(1)}, /*index=5*/bf16[112,128,128]{2,1,0:T(8,128)(2,1)}, ...), branch_computations={%region_25.28_spmd, %region_26.35_spmd} | conditional | flops 1494495232 | bytes 150286288 | solution.py:219
  1130.1 32.5 %conditional.2 = (bf16[64,5120]{1,0:T(8,128)(2,1)S(1)}) conditional(s32[]{:T(128)} %convert_element_type.159, bf16[64,5120]{1,0:T(8,128)(2,1)S(1)} %get-tuple-element.1015, (bf16[64,5120]{1,0:T(8,128)(2,1)S(1)}, bf16[2,64,5120]{2,1,0:T(8,128)(2,1)}, s32[]{:T(128)}, s32[112]{0:T(128)S(1)}, bf16[112,128,128]{2,1,0:T(8,128)(2,1)}, ...), branch_computations={%region_27.29_spmd, %region_28.32_spmd} | conditional | flops 747247680 | bytes 75143096 | solution.py:195
  1135.2 7.0 fusion.48
  1144.7 6.6 fusion.44
  1167.7 7.0 fusion.78
  1177.2 6.6 fusion.74
  1200.2 6.4 collective-permute-done.1
  1209.1 65.7 %conditional.7 = (bf16[64,5120]{1,0:T(8,128)(2,1)S(1)}, bf16[64,5120]{1,0:T(8,128)(2,1)S(1)}) conditional(s32[]{:T(128)} %convert_element_type.322, () %tuple.153, (s32[]{:T(128)}, bf16[64,5120]{1,0:T(8,128)(2,1)S(1)}, bf16[2,64,5120]{2,1,0:T(8,128)(2,1)}, s32[]{:T(128)}, s32[112]{0:T(128)S(1)}, /*index=5*/bf16[112,128,128]{2,1,0:T(8,128)(2,1)}, ...), branch_computations={%region_25.28_spmd, %region_26.35_spmd} | conditional | flops 1494495232 | bytes 150286288 | solution.py:219
  1209.8 32.5 %conditional.2 = (bf16[64,5120]{1,0:T(8,128)(2,1)S(1)}) conditional(s32[]{:T(128)} %convert_element_type.159, bf16[64,5120]{1,0:T(8,128)(2,1)S(1)} %get-tuple-element.1015, (bf16[64,5120]{1,0:T(8,128)(2,1)S(1)}, bf16[2,64,5120]{2,1,0:T(8,128)(2,1)}, s32[]{:T(128)}, s32[112]{0:T(128)S(1)}, bf16[112,128,128]{2,1,0:T(8,128)(2,1)}, ...), branch_computations={%region_27.29_spmd, %region_28.32_spmd} | conditional | flops 747247680 | bytes 75143096 | solution.py:195
  1214.8 7.0 fusion.48
  1224.3 6.6 fusion.44
  1247.3 7.0 fusion.78
  1256.8 6.6 fusion.74
  1279.9 6.4 collective-permute-done.1
  1298.4 7.3 fusion.121
  1314.2 7.3 fusion.128
  1324.7 12.9 convert_bitcast_fusion.5
  1337.6 13.3 fusion.112
  1354.7 7.6 copy.113
  1362.7 7.3 convert_bitcast_fusion.4
  1370.0 7.1 fusion.115
  1379.8 7.7 copy.116
  1387.5 76.7 %reduce-scatter.3.cloned.1.call-done = bf16[2,112,4,128]{3,1,0,2:T(8,128)(2,1)} async-done(((bf16[2,112,128,128]{3,1,0,2:T(8,128)(2,1)}), bf16[2,112,4,128]{3,1,0,2:T(8,128)(2,1)}) %reduce-scatter.3.cloned.1.call-update) | async-done | bytes 229392 | tf_op jit(solution)/shard_map/reduce_scatter | solution.py:239
  1465.9 97.7 %reduce-scatter.5.cloned.1.call-done = bf16[2,112,4,128]{3,1,0,2:T(8,128)(2,1)} async-done(((bf16[2,112,128,128]{3,1,0,2:T(8,128)(2,1)}), bf16[2,112,4,128]{3,1,0,2:T(8,128)(2,1)}) %reduce-scatter.5.cloned.1.call-update) | async-done | bytes 229392 | tf_op jit(solution)/shard_map/reduce_scatter | solution.py:242
  (498 shorter events, 403.2 us)
Async XLA Ops:
  7.2 63.9 %all-gather.3.cloned.1.call-start = ((), (), s32[]{:S(2)}) async-start(), calls=%async_computation.2 | async-start | bytes 7569408 | tf_op jit(solution)/shard_map/all_gather | solution.py:138
  8.9 120.3 %all-gather.5.cloned.1.call-start = ((), (), s32[]{:S(2)}) async-start(), calls=%async_computation.3 | async-start | bytes 7569408 | tf_op jit(solution)/shard_map/all_gather | solution.py:139
  10.6 1453.6 %reduce-scatter.3.cloned.1.call-start = ((), (), s32[]{:S(2)}) async-start(), calls=%async_computation.4 | async-start | bytes 7569408 | tf_op jit(solution)/shard_map/reduce_scatter | solution.py:239
  11.4 64.1 %copy-start.15 = (s32[112]{0:T(128)}, s32[112]{0:T(128)S(1)}, u32[]{:S(2)}) copy-start(s32[112]{0:T(128)S(1)} %get-tuple-element.1561) | copy-start | bytes 1348
  11.4 64.1 %copy-start.17 = (s32[112]{0:T(128)}, s32[112]{0:T(128)S(1)}, u32[]{:S(2)}) copy-start(s32[112]{0:T(128)S(1)} %get-tuple-element.1568) | copy-start | bytes 1348
  15.2 60.3 %copy-start.27 = (s32[120]{0:T(128)}, s32[120]{0:T(128)S(1)}, u32[]{:S(2)}) copy-start(s32[120]{0:T(128)S(1)} %select_n.203) | copy-start | bytes 1444
  15.7 59.8 %copy-start.29 = (s32[120]{0:T(128)}, s32[120]{0:T(128)S(1)}, u32[]{:S(2)}) copy-start(s32[120]{0:T(128)S(1)} %select_n.205) | copy-start | bytes 1444
  75.5 1.8 copy-start.4
  75.5 3.0 copy-start.5
  133.6 4.1 copy-start.9
  133.6 4.1 copy-start.10
  137.8 1.8 copy-start.1
  146.8 4.6 copy-start
  158.5 4.5 copy-start.11
  163.0 3.4 copy-start.12
  213.5 15.7 collective-permute-start
  270.3 17.6 %collective-permute-start = (bf16[64,5120]{1,0:T(8,128)(2,1)}, bf16[64,5120]{1,0:T(8,128)(2,1)S(1)}, u32[]{:S(2)}, u32[]{:S(2)}) collective-permute-start(bf16[64,5120]{1,0:T(8,128)(2,1)} %get-tuple-element.1449), channel_id=1, source_target_pairs={{0,32},{32,64},{64,96},{96,128},{128,160},{160,192},{192,224},{1,3... | collective-permute-start | bytes 1966088 | tf_op jit(solution)/shard_map/while/body/eval_jaxpr/ppermute | solution.py:16
  293.0 52.6 %collective-permute-start = (bf16[64,5120]{1,0:T(8,128)(2,1)}, bf16[64,5120]{1,0:T(8,128)(2,1)S(1)}, u32[]{:S(2)}, u32[]{:S(2)}) collective-permute-start(bf16[64,5120]{1,0:T(8,128)(2,1)} %get-tuple-element.1449), channel_id=1, source_target_pairs={{0,32},{32,64},{64,96},{96,128},{128,160},{160,192},{192,224},{1,3... | collective-permute-start | bytes 1966088 | tf_op jit(solution)/shard_map/while/body/eval_jaxpr/ppermute | solution.py:16
  350.7 15.8 %collective-permute-start = (bf16[64,5120]{1,0:T(8,128)(2,1)}, bf16[64,5120]{1,0:T(8,128)(2,1)S(1)}, u32[]{:S(2)}, u32[]{:S(2)}) collective-permute-start(bf16[64,5120]{1,0:T(8,128)(2,1)} %get-tuple-element.1449), channel_id=1, source_target_pairs={{0,32},{32,64},{64,96},{96,128},{128,160},{160,192},{192,224},{1,3... | collective-permute-start | bytes 1966088 | tf_op jit(solution)/shard_map/while/body/eval_jaxpr/ppermute | solution.py:16
  371.7 31.4 %collective-permute-start = (bf16[64,5120]{1,0:T(8,128)(2,1)}, bf16[64,5120]{1,0:T(8,128)(2,1)S(1)}, u32[]{:S(2)}, u32[]{:S(2)}) collective-permute-start(bf16[64,5120]{1,0:T(8,128)(2,1)} %get-tuple-element.1449), channel_id=1, source_target_pairs={{0,32},{32,64},{64,96},{96,128},{128,160},{160,192},{192,224},{1,3... | collective-permute-start | bytes 1966088 | tf_op jit(solution)/shard_map/while/body/eval_jaxpr/ppermute | solution.py:16
  408.2 14.4 collective-permute-start
  427.7 30.3 %collective-permute-start = (bf16[64,5120]{1,0:T(8,128)(2,1)}, bf16[64,5120]{1,0:T(8,128)(2,1)S(1)}, u32[]{:S(2)}, u32[]{:S(2)}) collective-permute-start(bf16[64,5120]{1,0:T(8,128)(2,1)} %get-tuple-element.1449), channel_id=1, source_target_pairs={{0,32},{32,64},{64,96},{96,128},{128,160},{160,192},{192,224},{1,3... | collective-permute-start | bytes 1966088 | tf_op jit(solution)/shard_map/while/body/eval_jaxpr/ppermute | solution.py:16
  463.2 14.1 collective-permute-start
  482.5 49.5 %collective-permute-start = (bf16[64,5120]{1,0:T(8,128)(2,1)}, bf16[64,5120]{1,0:T(8,128)(2,1)S(1)}, u32[]{:S(2)}, u32[]{:S(2)}) collective-permute-start(bf16[64,5120]{1,0:T(8,128)(2,1)} %get-tuple-element.1449), channel_id=1, source_target_pairs={{0,32},{32,64},{64,96},{96,128},{128,160},{160,192},{192,224},{1,3... | collective-permute-start | bytes 1966088 | tf_op jit(solution)/shard_map/while/body/eval_jaxpr/ppermute | solution.py:16
  553.6 5.2 copy-start.24
  563.3 5.2 copy-start.23
  572.9 2.6 copy-start.16
  572.9 2.6 copy-start.18
  572.9 2.6 copy-start.28
  572.9 2.6 copy-start.30
  577.1 1.0 copy-start.6
  578.2 13.3 copy-start.7
  578.2 13.3 collective-permute-start.1
  593.0 1.0 copy-start.6
  594.2 28.2 %copy-start.7 = (bf16[2,64,5120]{2,1,0:T(8,128)(2,1)S(1)}, bf16[2,64,5120]{2,1,0:T(8,128)(2,1)}, u32[]{:S(2)}) copy-start(bf16[2,64,5120]{2,1,0:T(8,128)(2,1)} %copy-done.6) | copy-start | bytes 3932164 | tf_op jit(solution)/shard_map/while
  594.2 28.2 %collective-permute-start.1 = (bf16[64,5120]{1,0:T(8,128)(2,1)S(1)}, bf16[64,5120]{1,0:T(8,128)(2,1)S(1)}, u32[]{:S(2)}, u32[]{:S(2)}) collective-permute-start(bf16[64,5120]{1,0:T(8,128)(2,1)S(1)} %get-tuple-element.1478), channel_id=1, source_target_pairs={{32,0},{64,32},{96,64},{128,96},{160,128},{192,160},{224,192},{33,... | collective-permute-start | bytes 1966088 | tf_op jit(solution)/shard_map/while/body/eval_jaxpr/ppermute | solution.py:16
  625.0 13.3 copy-start.7
  625.0 13.3 collective-permute-start.1
  640.9 45.9 %copy-start.7 = (bf16[2,64,5120]{2,1,0:T(8,128)(2,1)S(1)}, bf16[2,64,5120]{2,1,0:T(8,128)(2,1)}, u32[]{:S(2)}) copy-start(bf16[2,64,5120]{2,1,0:T(8,128)(2,1)} %copy-done.6) | copy-start | bytes 3932164 | tf_op jit(solution)/shard_map/while
  640.9 45.8 %collective-permute-start.1 = (bf16[64,5120]{1,0:T(8,128)(2,1)S(1)}, bf16[64,5120]{1,0:T(8,128)(2,1)S(1)}, u32[]{:S(2)}, u32[]{:S(2)}) collective-permute-start(bf16[64,5120]{1,0:T(8,128)(2,1)S(1)} %get-tuple-element.1478), channel_id=1, source_target_pairs={{32,0},{64,32},{96,64},{128,96},{160,128},{192,160},{224,192},{33,... | collective-permute-start | bytes 1966088 | tf_op jit(solution)/shard_map/while/body/eval_jaxpr/ppermute | solution.py:16
  689.4 13.2 copy-start.7
  689.4 13.2 collective-permute-start.1
  705.2 46.2 %copy-start.7 = (bf16[2,64,5120]{2,1,0:T(8,128)(2,1)S(1)}, bf16[2,64,5120]{2,1,0:T(8,128)(2,1)}, u32[]{:S(2)}) copy-start(bf16[2,64,5120]{2,1,0:T(8,128)(2,1)} %copy-done.6) | copy-start | bytes 3932164 | tf_op jit(solution)/shard_map/while
  705.2 46.2 %collective-permute-start.1 = (bf16[64,5120]{1,0:T(8,128)(2,1)S(1)}, bf16[64,5120]{1,0:T(8,128)(2,1)S(1)}, u32[]{:S(2)}, u32[]{:S(2)}) collective-permute-start(bf16[64,5120]{1,0:T(8,128)(2,1)S(1)} %get-tuple-element.1478), channel_id=1, source_target_pairs={{32,0},{64,32},{96,64},{128,96},{160,128},{192,160},{224,192},{33,... | collective-permute-start | bytes 1966088 | tf_op jit(solution)/shard_map/while/body/eval_jaxpr/ppermute | solution.py:16
  754.0 372.9 %copy-start.7 = (bf16[2,64,5120]{2,1,0:T(8,128)(2,1)S(1)}, bf16[2,64,5120]{2,1,0:T(8,128)(2,1)}, u32[]{:S(2)}) copy-start(bf16[2,64,5120]{2,1,0:T(8,128)(2,1)} %copy-done.6) | copy-start | bytes 3932164 | tf_op jit(solution)/shard_map/while
  754.0 372.9 %collective-permute-start.1 = (bf16[64,5120]{1,0:T(8,128)(2,1)S(1)}, bf16[64,5120]{1,0:T(8,128)(2,1)S(1)}, u32[]{:S(2)}, u32[]{:S(2)}) collective-permute-start(bf16[64,5120]{1,0:T(8,128)(2,1)S(1)} %get-tuple-element.1478), channel_id=1, source_target_pairs={{32,0},{64,32},{96,64},{128,96},{160,128},{192,160},{224,192},{33,... | collective-permute-start | bytes 1966088 | tf_op jit(solution)/shard_map/while/body/eval_jaxpr/ppermute | solution.py:16
  1156.4 2.7 copy-start.2
  1188.9 2.7 copy-start.3
  1195.1 11.5 copy-start.7
  1195.1 11.5 collective-permute-start.1
  1236.0 2.7 copy-start.2
  1268.5 2.7 copy-start.3
  1274.8 11.5 copy-start.7
  1274.8 11.5 collective-permute-start.1
  1286.9 3.5 copy-start.19
  1286.9 3.6 copy-start.8
  1287.2 3.9 copy-start.22
  1290.5 1.7 copy-start.13
  1294.0 4.4 copy-start.20
  1311.2 3.0 copy-start.21
  1321.5 3.2 copy-start.26
  1324.7 12.9 copy-start.25
  1362.4 201.2 %reduce-scatter.5.cloned.1.call-start = ((), (), s32[]{:S(2)}) async-start(), calls=%async_computation.5 | async-start | bytes 7569408 | tf_op jit(solution)/shard_map/reduce_scatter | solution.py:242
  1362.7 7.3 copy-start.14
  (7 other events, 7.2 us)
Sparse Core Ops, SparseCore 0:
  11.1 59.9 all-gather.2
  74.2 54.9 all-gather.4
  1362.5 101.6 reduce-scatter.2
  1468.1 95.4 reduce-scatter.4
where the time goes:
time: 1560 us; the launch traced here: 1570 us
  waiting for transfers between devices  844 us (54%)
  local copies, waits for them, and re-layouts  247 us (16%)
  starting transfers between devices  153 us (10%)
  other arithmetic  147 us (9%)
  matrix products  146 us (9%)
  loops' own time  18.9 us (1%)
    ppermute x18, waiting for transfers between devices, passed_along(): lax.ppermute(value, axis, [(source, source + steps) for source in range(f...  575 us
    ppermute x18, starting transfers between devices, passed_along(): lax.ppermute(value, axis, [(source, source + steps) for source in range(f...  153 us
    reduce_scatter x1, waiting for transfers between devices, local(): lax.psum_scatter(jnp.stack([down_one, down_two]).astype(jnp.bfloat16), 'd...  97.7 us
    reduce_scatter x1, waiting for transfers between devices, local(): lax.psum_scatter(jnp.stack([up_one, up_two]).astype(jnp.bfloat16), 'dp',...  76.7 us
    dynamic_update_slice x36, other arithmetic, put(): lax.dynamic_update_index_in_dim(buffer, jnp.where(is_live, value, older),...  60.4 us
    dot_general x10, matrix products, layer_parts(): jnp.einsum('rfi,fio->rfo', picked, w_up, preferred_element_type=jnp.float32)  55.5 us
    dynamic_slice x54, local copies, waits for them, and re-layouts, put(): older = lax.dynamic_index_in_dim(buffer, slot_idx, 0, keepdims=False)  51.5 us
    all_gather x1, waiting for transfers between devices, local(): lax.all_gather(up_blocks, 'dp', axis=2, tiled=True)  48.4 us
  transfers between devices with their start and end apart: 22, of which 22 were waited for; matrix products, arithmetic and copies ran while one was open for 7% of the time, Pallas kernels for 0%

commit v1 on v0

v1 whole, which is shorter than its diff:
```python
import functools

import jax
import jax.numpy as jnp
from jax import lax
from jax.experimental import pallas as pl
from jax.experimental.pallas import tpu as pltpu
from jax.sharding import PartitionSpec as P

GROUPS = 4
UNROLL = 28
EPS = 1e-05
SIDE = 4

root_coef = 0.7978845608028654
cubic_coef = 0.044715

HBM = pl.BlockSpec(memory_space=pltpu.HBM)
SMEM = pl.BlockSpec(memory_space=pltpu.SMEM)
NN = (((1,), (0,)), ((), ()))
NT = (((1,), (1,)), ((), ()))
TN = (((0,), (0,)), ((), ()))


def dot(a, b, dims):
    return lax.dot_general(a, b, dims, preferred_element_type=jnp.float32)


def gelu_parts(p):
    square = p * p
    tangent = jnp.tanh(p * (root_coef + (root_coef * cubic_coef) * square))
    half = 0.5 * p
    gate = 0.5 + 0.5 * tangent
    slope = gate + half * (1.0 - tangent * tangent) * (
        root_coef + (3.0 * root_coef * cubic_coef) * square
    )
    return p * gate, slope


def lanes(block):
    return pl.ds(pl.multiple_of(block * 128, 128), 128)


def each_block(count, body, init, step=10):
    def run(i, carry):
        for u in range(step):
            carry = body(i * step + u, carry)
        return carry

    return lax.fori_loop(0, count // step, run, init)


def inverse_rms(h):
    rows, width = h.shape

    def add(k, totals):
        value = h[:, lanes(k)].astype(jnp.float32)
        return totals[1], totals[0] + value * value

    zero = jnp.zeros((rows, 128), jnp.float32)
    one, two = each_block(width // 128, add, (zero, zero))
    return lax.rsqrt(jnp.sum(one + two, axis=1, keepdims=True) * (1.0 / width) + EPS)


def weight_copy(weights, held, sems, l, which, j):
    count = weights.shape[0] // 4
    part = pl.ds((2 * l + which) * count + j * UNROLL, UNROLL)
    return pltpu.make_async_copy(weights.at[part], held.at[part], sems.at[l, which, j])


def load_weights(weights, held, sems, l):
    for j in range(weights.shape[0] // 4 // UNROLL):
        for which in range(2):
            weight_copy(weights, held, sems, l, which, j).start()


def run_pairs(count, before, body):
    def group(j, _):
        before(j)
        for u in range(0, UNROLL, 2):
            body(j * UNROLL + u)
        return 0

    lax.fori_loop(0, count // UNROLL, group, 0)


def pair_dot(left, right, weights, dims):
    rows = left.shape[0]
    both = jnp.concatenate([left, right], axis=0)
    axis = 1 if dims is NN else 0
    wide = dot(both, jnp.concatenate(weights, axis=axis), dims)
    return wide[:rows, :128], wide[rows:, 128:]


def forward_kernel(tick, meta, ups, downs, tok, inc, weights, after, *refs):
    (_, _, _, _, _, y, kin, kmid, kout, slope, gated,
     xv, held, normed, acc, sv, gv, wsem, ssem, gsem, iosem) = refs
    section = meta[0]
    mb = tick - section
    live = (mb >= 0) & (mb < GROUPS)
    layers = meta[1]
    two = layers > 1
    count, width = ups.shape[1], xv.shape[2]

    def io(n, src, dst):
        return pltpu.make_async_copy(src, dst, iosem.at[n])

    def save_slope(l):
        return pltpu.make_async_copy(sv.at[l], slope.at[l, :, mb], ssem.at[l])

    def save_gated(l):
        return pltpu.make_async_copy(gv.at[l], gated.at[l, :, mb], gsem.at[l])

    def layer(l, _):
        x, out = xv.at[l], xv.at[l + 1]
        inv = inverse_rms(x)

        def start(k, _):
            value = x[:, lanes(k)].astype(jnp.float32)
            normed[:, lanes(k)] = (value * inv).astype(jnp.bfloat16)
            acc[:, lanes(k)] = value
            return 0

        each_block(width // 128, start, 0)
        up_at, down_at = 2 * l * count, (2 * l + 1) * count

        def body(f):
            pres = pair_dot(
                normed[:, lanes(ups[l, f])],
                normed[:, lanes(ups[l, f + 1])],
                (held[up_at + f], held[up_at + f + 1]),
                NN,
            )
            values = []
            for q, pre in enumerate(pres):
                value, grad = gelu_parts(pre)
                values.append(value.astype(jnp.bfloat16))
                gv[l, f + q] = values[q]
                sv[l, f + q] = grad.astype(jnp.bfloat16)
            mixed = pair_dot(
                *values, (held[down_at + f], held[down_at + f + 1]), NN
            )
            for q in range(2):
                at = lanes(downs[l, f + q])
                acc[:, at] = acc[:, at] + mixed[q]

        def before(j):
            for which in range(2):
                weight_copy(weights, held, wsem, l, which, j).wait()

        run_pairs(count, before, body)
        save_slope(l).start()
        save_gated(l).start()

        def finish(k, _):
            out[:, lanes(k)] = acc[:, lanes(k)].astype(jnp.bfloat16)
            return 0

        each_block(width // 128, finish, 0)
        return 0

    @pl.when(live)
    def _():
        @pl.when(section == 0)
        def _():
            io(0, tok.at[mb], xv.at[0]).start()

        @pl.when(section != 0)
        def _():
            io(0, inc, xv.at[0]).start()

        load_weights(weights, held, wsem, 0)

        @pl.when(two)
        def _():
            load_weights(weights, held, wsem, 1)

        io(0, inc, xv.at[0]).wait()
        io(1, xv.at[0], kin.at[mb]).start()
        lax.fori_loop(0, layers, layer, 0)
        io(2, xv.at[layers], y).start()
        io(3, xv.at[layers], kout.at[mb]).start()

        @pl.when(two)
        def _():
            io(4, xv.at[1], kmid.at[mb]).start()
            io(4, xv.at[1], kmid.at[mb]).wait()
            save_slope(1).wait()
            save_gated(1).wait()

        io(2, xv.at[layers], y).wait()
        io(3, xv.at[layers], kout.at[mb]).wait()
        io(1, xv.at[0], kin.at[mb]).wait()
        save_slope(0).wait()
        save_gated(0).wait()


def backward_kernel(tick, last, meta, ups, downs, cotg, inc, weights, kin, kmid, slope, *refs):
    (_, _, _, _, dx, kdx, ktop, kinner, dpre,
     cv, hv, held, acc, sv, dv, wsem, ssem, dsem, iosem) = refs
    section = meta[0]
    mb = tick - (last - section)
    live = (mb >= 0) & (mb < GROUPS)
    layers = meta[1]
    two = layers > 1
    count, width = ups.shape[1], cv.shape[2]
    rows = cv.shape[1]

    def io(n, src, dst):
        return pltpu.make_async_copy(src, dst, iosem.at[n])

    def load_slope(l):
        return pltpu.make_async_copy(slope.at[l, :, mb], sv.at[l], ssem.at[l])

    def save_dpre(l):
        return pltpu.make_async_copy(dv.at[l], dpre.at[l, :, mb], dsem.at[l])

    def load_hidden(l, kept):
        return io(1 + l, kept.at[mb], hv.at[l])

    def layer(i, _):
        l = layers - 1 - i
        h, cot, out = hv.at[l], cv.at[l + 1], cv.at[l]
        load_hidden(l, kin).wait()
        inv = inverse_rms(h)

        def blank(k, _):
            acc[:, lanes(k)] = jnp.zeros((rows, 128), jnp.float32)
            return 0

        each_block(width // 128, blank, 0)
        load_slope(l).wait()
        up_at, down_at = 2 * l * count, (2 * l + 1) * count

        def body(f):
            inners = pair_dot(
                cot[:, lanes(downs[l, f])],
                cot[:, lanes(downs[l, f + 1])],
                (held[down_at + f], held[down_at + f + 1]),
                NT,
            )
            values = []
            for q, inner in enumerate(inners):
                scaled = inner * sv[l, f + q].astype(jnp.float32)
                values.append(scaled.astype(jnp.bfloat16))
                dv[l, f + q] = values[q]
            mixed = pair_dot(*values, (held[up_at + f], held[up_at + f + 1]), NT)
            for q in range(2):
                at = lanes(ups[l, f + q])
                acc[:, at] = acc[:, at] + mixed[q]

        def before(j):
            for which in range(2):
                weight_copy(weights, held, wsem, l, which, j).wait()

        run_pairs(count, before, body)
        save_dpre(l).start()

        def dots(k, totals):
            value = acc[:, lanes(k)] * h[:, lanes(k)].astype(jnp.float32)
            return totals[1], totals[0] + value

        zero = jnp.zeros((rows, 128), jnp.float32)
        one, other = each_block(width // 128, dots, (zero, zero))
        mean = jnp.sum(one + other, axis=1, keepdims=True) * inv * (1.0 / width)

        def finish(k, _):
            normal = h[:, lanes(k)].astype(jnp.float32) * inv
            value = cot[:, lanes(k)].astype(jnp.float32) + inv * (
                acc[:, lanes(k)] - normal * mean
            )
            out[:, lanes(k)] = value.astype(jnp.bfloat16)
            return 0

        each_block(width // 128, finish, 0)
        return 0

    @pl.when(live)
    def _():
        @pl.when(section == last)
        def _():
            io(0, cotg.at[mb], cv.at[layers]).start()

        @pl.when(section != last)
        def _():
            io(0, inc, cv.at[layers]).start()

        @pl.when(two)
        def _():
            load_hidden(1, kmid).start()
            load_slope(1).start()
            load_weights(weights, held, wsem, 1)

        load_hidden(0, kin).start()
        load_slope(0).start()
        load_weights(weights, held, wsem, 0)
        io(0, inc, cv.at[layers]).wait()
        lax.fori_loop(0, layers, layer, 0)
        io(5, cv.at[0], dx).start()
        io(6, cv.at[0], kdx.at[mb]).start()
        io(4, cv.at[1], kinner.at[mb]).start()

        @pl.when(two)
        def _():
            io(3, cv.at[2], ktop.at[mb]).start()
            io(3, cv.at[2], ktop.at[mb]).wait()
            save_dpre(1).wait()

        io(5, cv.at[0], dx).wait()
        io(6, cv.at[0], kdx.at[mb]).wait()
        io(4, cv.at[1], kinner.at[mb]).wait()
        save_dpre(0).wait()


def grad_kernel(l, meta, ups, downs, h, cot, gated, dpre, keep, send, normed):
    step = pl.program_id(0)
    count = keep.shape[2]
    width = h.shape[1]
    active = meta[1] > l

    @pl.when(active)
    def _():
        @pl.when(step == 0)
        def _():
            inv = inverse_rms(h)

            def start(k, _):
                normed[:, lanes(k)] = (h[:, lanes(k)].astype(jnp.float32) * inv).astype(
                    jnp.bfloat16
                )
                return 0

            each_block(width // 128, start, 0, 2)

        is_zero = meta[4] == 0
        for u in range(count):
            f = step * count + u
            up = dot(normed[:, lanes(ups[l, f])], dpre[0, u], TN)
            down = dot(gated[0, u], cot[:, lanes(downs[l, f])], TN)
            mine = jnp.where(is_zero, up, down).astype(jnp.bfloat16)
            other = jnp.where(is_zero, down, up).astype(jnp.bfloat16)
            for i in range(SIDE):
                for j in range(SIDE):
                    rows = slice((i * SIDE + j) * 8, (i * SIDE + j) * 8 + 8)
                    keep[i ^ meta[2], j ^ meta[3], u] = mine[rows]
                    send[i ^ meta[2], j ^ meta[3], u] = other[rows]

    @pl.when(jnp.logical_not(active))
    def _():
        keep[...] = jnp.zeros_like(keep)
        send[...] = jnp.zeros_like(send)


def block_grads(l, meta, ups, downs, h, cot, gated, dpre):
    count, width = ups.shape[1], h.shape[1]
    rows, per = h.shape[0], 14
    whole = pl.BlockSpec((rows, width), lambda i: (0, 0))
    table = pl.BlockSpec((1, per, rows, 128), lambda i: (l, i, 0, 0))
    out = pl.BlockSpec((SIDE, SIDE, per, 8, 128), lambda i: (0, 0, i, 0, 0))
    shape = jax.ShapeDtypeStruct((SIDE, SIDE, count, 8, 128), jnp.bfloat16)
    return pl.pallas_call(
        functools.partial(grad_kernel, l),
        grid=(count // per,),
        in_specs=[SMEM, SMEM, SMEM, whole, whole, table, table],
        out_specs=[out, out],
        out_shape=[shape, shape],
        scratch_shapes=[pltpu.VMEM((rows, width), jnp.bfloat16)],
        compiler_params=pltpu.CompilerParams(vmem_limit_bytes=56 << 20),
        name="grads",
    )(meta, ups, downs, h, cot, gated, dpre)


def swap(value, change):
    pairs = []
    for x in range(SIDE):
        for y in range(SIDE):
            for c in range(2):
                a, b, d = change(x, y, c)
                pairs.append(((x * SIDE + y) * 2 + c, (a * SIDE + b) * 2 + d))
    return lax.ppermute(value, "dp", pairs)


def along(axis, bits):
    if axis == 0:
        return lambda x, y, c: (x ^ bits, y, c)
    return lambda x, y, c: (x, y ^ bits, c)


def add(a, b):
    return (a.astype(jnp.float32) + b.astype(jnp.float32)).astype(jnp.bfloat16)


def other_core(value):
    return swap(value, lambda x, y, c: (x, y, 1 - c))


def parts(value, axis, picks):
    return jnp.concatenate(
        [lax.slice_in_dim(value, p, p + 1, axis=axis) for p in picks], axis=axis
    )


def scatter_sum(first, second):
    half = first.shape[2] // 2
    colors = [
        (first[:, :, :half], (1, 0), 1),
        (first[:, :, half:], (1, 0), 3),
        (second[:, :, :half], (0, 1), 1),
        (second[:, :, half:], (0, 1), 3),
    ]
    values = [c[0] for c in colors]
    for stage in range(4):
        fresh = []
        for value, (_, axes, bits) in zip(values, colors):
            axis = axes[stage // 2]
            if stage % 2 == 0:
                send = parts(value, axis, (bits, 2))
                keep = parts(value, axis, (0, bits ^ 2))
                got = swap(send, along(axis, bits))
            else:
                send = parts(value, axis, (1,))
                keep = parts(value, axis, (0,))
                got = swap(send, along(axis, bits ^ 2))
            fresh.append(add(keep, got))
        values = fresh
    shape = (2 * half,) + first.shape[3:]
    return (
        jnp.concatenate(values[:2], axis=2).reshape(shape),
        jnp.concatenate(values[2:], axis=2).reshape(shape),
    )


def blank_arrays(*shapes):
    def kernel(*refs):
        pass

    return pl.pallas_call(
        kernel,
        out_shape=[jax.ShapeDtypeStruct(s, jnp.bfloat16) for s in shapes],
        out_specs=[HBM] * len(shapes),
        name="blank",
    )()


def relay(value, live, steps):
    return lax.ppermute(value, "section", [(s, s + steps) for s in live])


def local(sections, tokens, cotangent, section_layers, up_rows, down_cols, up_blocks, down_blocks):
    last = sections - 1
    tok_rows, width = tokens.shape
    count = up_rows.shape[1]
    groups, rows = GROUPS, tok_rows // GROUPS
    place = lax.axis_index("dp").astype(jnp.int32)
    core = place % 2
    meta = jnp.stack(
        [
            lax.axis_index("section").astype(jnp.int32),
            section_layers[0],
            place // (2 * SIDE),
            (place // 2) % SIDE,
            core,
        ]
    )
    shares = jnp.stack([up_blocks, down_blocks], axis=1).reshape(
        (4 * count,) + up_blocks.shape[2:]
    )
    weights = lax.all_gather(shares, "dp", axis=0)
    weights = jnp.swapaxes(weights, 0, 1).reshape(4 * count, 128, 128)
    tok = tokens.reshape(groups, rows, width)
    cotg = cotangent.reshape(groups, rows, width)
    act = (groups, rows, width)
    table = (2, count, groups, rows, 128)
    bf16 = jnp.bfloat16
    one = jax.ShapeDtypeStruct((rows, width), bf16)
    act_s, table_s = jax.ShapeDtypeStruct(act, bf16), jax.ShapeDtypeStruct(table, bf16)
    dma = pltpu.SemaphoreType.DMA
    params = pltpu.CompilerParams(vmem_limit_bytes=56 << 20)
    flops = 8 * rows * count * 128 * 128
    cost = pl.CostEstimate(flops=flops, bytes_accessed=16 << 20, transcendentals=0)

    def forward(tick, incoming, after, state):
        return pl.pallas_call(
            functools.partial(forward_kernel, tick),
            in_specs=[SMEM] * 3 + [HBM] * 9,
            out_specs=[HBM] * 6,
            out_shape=[one, act_s, act_s, act_s, table_s, table_s],
            scratch_shapes=[
                pltpu.VMEM((3, rows, width), bf16),
                pltpu.VMEM((4 * count, 128, 128), bf16),
                pltpu.VMEM((rows, width), bf16),
                pltpu.VMEM((rows, width), jnp.float32),
                pltpu.VMEM((2, count, rows, 128), bf16),
                pltpu.VMEM((2, count, rows, 128), bf16),
                dma((2, 2, count // UNROLL)),
                dma((2,)),
                dma((2,)),
                dma((5,)),
            ],
            input_output_aliases={7 + i: 1 + i for i in range(5)},
            compiler_params=params,
            cost_estimate=cost,
            name="forward",
        )(meta, up_rows, down_cols, tok, incoming, weights, after, *state)

    def backward(tick, incoming, saved, state):
        return pl.pallas_call(
            functools.partial(backward_kernel, tick, last),
            in_specs=[SMEM] * 3 + [HBM] * 10,
            out_specs=[HBM] * 5,
            out_shape=[one, act_s, act_s, act_s, table_s],
            scratch_shapes=[
                pltpu.VMEM((3, rows, width), bf16),
                pltpu.VMEM((2, rows, width), bf16),
                pltpu.VMEM((4 * count, 128, 128), bf16),
                pltpu.VMEM((rows, width), jnp.float32),
                pltpu.VMEM((2, count, rows, 128), bf16),
                pltpu.VMEM((2, count, rows, 128), bf16),
                dma((2, 2, count // UNROLL)),
                dma((2,)),
                dma((2,)),
                dma((7,)),
            ],
            input_output_aliases={9 + i: 1 + i for i in range(4)},
            compiler_params=params,
            cost_estimate=cost,
            name="backward",
        )(meta, up_rows, down_cols, cotg, incoming, weights, *saved, *state)

    empty, *state = blank_arrays((rows, width), act, act, act, table, table)
    incoming, after = empty, empty
    grad_empty, *grad_state = blank_arrays((rows, width), act, act, act, table)
    grad_incoming = grad_empty
    for tick in range(groups + 2 * last):
        if tick < groups + last:
            result, *state = forward(tick, incoming, after, state)
            live = [s for s in range(last) if 0 <= tick - s < groups]
            if live:
                incoming = relay(result, live, 1)
        back = tick - last
        if back >= 0:
            kin, kmid, _, slope, _ = state
            result, *grad_state = backward(back, grad_incoming, (kin, kmid, slope), grad_state)
            after = result
            live = [s for s in range(1, sections) if 0 <= back - (last - s) < groups]
            if live:
                grad_incoming = relay(result, live, -1)
    kin, kmid, kout, slope, gated = state
    kdx, ktop, kinner, dpre = grad_state

    def flat(a):
        return a.reshape(tok_rows, width)

    gated = gated.reshape(2, count, tok_rows, 128)
    dpre = dpre.reshape(2, count, tok_rows, 128)
    totals = []
    for l, h, cot in ((1, kmid, ktop), (0, kin, kinner)):
        keep, send = block_grads(l, meta, up_rows, down_cols, flat(h), flat(cot), gated, dpre)
        totals.append(add(keep, other_core(send)))
    late, early = scatter_sum(*totals)
    summed = jnp.stack([early, late])
    low, high = summed[:, :, :4], summed[:, :, 4:]
    mine = jnp.where(core == 0, low, high)
    theirs = other_core(jnp.where(core == 0, high, low))
    return (
        kout.reshape(1, tok_rows, width),
        kdx.reshape(1, tok_rows, width),
        jnp.where(core == 0, mine, theirs),
        jnp.where(core == 0, theirs, mine),
    )


def solution(mesh):
    in_specs = (
        P("dp", None),
        P("dp", None),
        P("section"),
        P("section", None),
        P("section", None),
        P("section", None, "dp", None),
        P("section", None, "dp", None),
    )
    out_specs = (
        P("section", "dp", None),
        P("section", "dp", None),
        P("section", None, "dp", None),
        P("section", None, "dp", None),
    )
    step = functools.partial(local, mesh.shape["section"])
    return jax.shard_map(step, mesh=mesh, in_specs=in_specs, out_specs=out_specs, check_vma=False)
```

time: 1560 us -> 616 us (0.39); the launches traced: 1570 us -> 607 us
  waiting for transfers between devices: 844 us -> 375 us
  local copies, waits for them, and re-layouts: 247 us -> 33.8 us
  matrix products: 146 us -> 0 us
  other arithmetic: 147 us -> 12.2 us
  Pallas kernels: 0 us -> 102 us
  starting transfers between devices: 153 us -> 67.6 us
  loops' own time: 18.9 us -> 0 us
    ppermute x18 -> x39, waiting for transfers between devices: 575 us -> 298 us  [the longest x20 272 us: relay(): return lax.ppermute(value, 'section', [(s, s + steps) for s in live])]
    reduce_scatter x2 -> x0, waiting for transfers between devices: 174 us -> none  [the longest x1 97.7 us: local(): lax.psum_scatter(jnp.stack([down_one, down_two]).astype(jnp.bfloat16), 'd...]
    dot_general x26 -> x0, matrix products: 146 us -> none  [the longest x10 55.5 us: layer_parts(): jnp.einsum('rfi,fio->rfo', picked, w_up, preferred_element_type=jnp.float32)]
    pallas_call x0 -> x26, Pallas kernels: none -> 102 us  [the longest x11 42.1 us: backward(): pl.pallas_call(functools.partial(backward_kernel, tick, last), in_specs=[...]
    ppermute x18 -> x39, starting transfers between devices: 153 us -> 67.6 us  [the longest x19 40.7 us: swap(): return lax.ppermute(value, 'dp', pairs)]
    gather x28 -> x0, local copies, waits for them, and re-layouts: 77.3 us -> none  [the longest x10 19.3 us: layer_parts(): jnp.take(normed.reshape(count_rows, width // block, block), row_ids, axis=1)]
    dynamic_update_slice x36 -> x0, other arithmetic: 60.4 us -> none  [put(): lax.dynamic_update_index_in_dim(buffer, jnp.where(is_live, value, older),...]
    dynamic_slice x54 -> x0, local copies, waits for them, and re-layouts: 51.5 us -> none  [put(): older = lax.dynamic_index_in_dim(buffer, slot_idx, 0, keepdims=False)]
  transfers between devices with their start and end apart: 22 -> 40, of which waited for: 22 -> 20; matrix products, arithmetic and copies ran while one was open for 7% -> 2% of each run, Pallas kernels for 0% -> 3%
where the time goes in v1:
time: 616 us; the launch traced here: 607 us
  waiting for transfers between devices  375 us (61%)
  Pallas kernels  102 us (17%)
  starting transfers between devices  67.6 us (11%)
  local copies, waits for them, and re-layouts  33.8 us (5%)
  between operations  16.1 us (3%)
  other arithmetic  12.2 us (2%)
    ppermute x20, waiting for transfers between devices, relay(): return lax.ppermute(value, 'section', [(s, s + steps) for s in live])  272 us
    all_gather x1, waiting for transfers between devices, local(): weights = lax.all_gather(shares, 'dp', axis=0)  77.5 us
    pallas_call x11, Pallas kernels, backward(): pl.pallas_call(functools.partial(backward_kernel, tick, last), in_specs=[...  42.1 us
    ppermute x19, starting transfers between devices, swap(): return lax.ppermute(value, 'dp', pairs)  40.7 us
    pallas_call x11, Pallas kernels, forward(): pl.pallas_call(functools.partial(forward_kernel, tick), in_specs=[SMEM] *...  38.6 us
    ppermute x20, starting transfers between devices, relay(): return lax.ppermute(value, 'section', [(s, s + steps) for s in live])  26.9 us
    ppermute x19, waiting for transfers between devices, swap(): return lax.ppermute(value, 'dp', pairs)  26 us
    pallas_call x2, Pallas kernels, block_grads(): pl.pallas_call(functools.partial(grad_kernel, l), grid=(count // per,), i...  21.5 us
  transfers between devices with their start and end apart: 40, of which 20 were waited for; matrix products, arithmetic and copies ran while one was open for 2% of the time, Pallas kernels for 3%

profile of v1, /device:TPU:1, one launch (start us, length us, event | category | flops | bytes accessed | tf_op | source)
XLA Modules:
  0.0 607.2 jit_solution(7996509824949033753)
XLA Ops:
  7.2 1.1 copy_bitcast_fusion
  10.6 77.5 %all-gather.2.cloned.1.call-done = bf16[32,448,4,128]{3,1,2,0:T(8,128)(2,1)} async-done(((bf16[1,448,4,128]{3,1,2,0:T(8,128)(2,1)}), bf16[32,448,4,128]{3,1,2,0:T(8,128)(2,1)}) %all-gather.2.cloned.1.call-update) | async-done | bytes 14680080 | tf_op jit(solution)/shard_map/all_gather | solution.py:468
  88.1 14.9 %copy.115 = bf16[448,32,4,128]{3,2,1,0:T(4,128)(2,1)} copy(bf16[448,32,4,128]{3,0,2,1:T(8,128)(2,1)} %bitcast.79) | data formatting | bytes 29360128 | tf_op jit(solution)/shard_map/transpose | solution.py:469
  103.0 8.0 %forward.11 = (bf16[32,5120]{1,0:T(8,128)(2,1)}, bf16[4,32,5120]{2,1,0:T(8,128)(2,1)}, bf16[4,32,5120]{2,1,0:T(8,128)(2,1)}, bf16[4,32,5120]{2,1,0:T(8,128)(2,1)...) custom-call(s32[5]{0:T(128)} %stack.31.meta, ...), custom_call_target="tpu_custom_call", output_to_operand_aliasing={{1}: (7, {}), {2}: (8, {}), {3}: (9, {}), {4}: (10, {}), {5... | custom-call | flops 469762048 | bytes 16777216 | tf_op jit(solution)/shard_map/forward/pallas_call | solution.py:483
  111.0 1.3 collective-permute-start
  112.3 7.4 %collective-permute-done.inc = bf16[32,5120]{1,0:T(8,128)(2,1)S(1)} collective-permute-done((bf16[32,5120]{1,0:T(8,128)(2,1)}, bf16[32,5120]{1,0:T(8,128)(2,1)S(1)}, u32[]{:S(2)}, u32[]{:S(2)}) %collective-permute-start) | collective-permute-done | bytes 327712 | tf_op jit(solution)/shard_map/ppermute | solution.py:446
  120.4 8.0 %forward.12 = (bf16[32,5120]{1,0:T(8,128)(2,1)}, bf16[4,32,5120]{2,1,0:T(8,128)(2,1)}, bf16[4,32,5120]{2,1,0:T(8,128)(2,1)}, bf16[4,32,5120]{2,1,0:T(8,128)(2,1)...) custom-call(s32[5]{0:T(128)} %stack.31.meta, ...), custom_call_target="tpu_custom_call", output_to_operand_aliasing={{1}: (7, {}), {2}: (8, {}), {3}: (9, {}), {4}: (10, {}), {5... | custom-call | flops 469762048 | bytes 16777216 | tf_op jit(solution)/shard_map/forward/pallas_call | solution.py:483
  128.5 4.0 collective-permute-start.1
  132.5 6.5 %collective-permute-done.1.inc = bf16[32,5120]{1,0:T(8,128)(2,1)S(1)} collective-permute-done((bf16[32,5120]{1,0:T(8,128)(2,1)}, bf16[32,5120]{1,0:T(8,128)(2,1)S(1)}, u32[]{:S(2)}, u32[]{:S(2)}) %collective-permute-start.1) | collective-permute-done | bytes 327712 | tf_op jit(solution)/shard_map/ppermute | solution.py:446
  139.7 8.0 %forward.13 = (bf16[32,5120]{1,0:T(8,128)(2,1)}, bf16[4,32,5120]{2,1,0:T(8,128)(2,1)}, bf16[4,32,5120]{2,1,0:T(8,128)(2,1)}, bf16[4,32,5120]{2,1,0:T(8,128)(2,1)...) custom-call(s32[5]{0:T(128)} %stack.31.meta, ...), custom_call_target="tpu_custom_call", output_to_operand_aliasing={{1}: (7, {}), {2}: (8, {}), {3}: (9, {}), {4}: (10, {}), {5... | custom-call | flops 469762048 | bytes 16777216 | tf_op jit(solution)/shard_map/forward/pallas_call | solution.py:483
  147.7 4.0 collective-permute-start.2
  151.8 5.7 collective-permute-done.2.inc
  158.1 8.0 %forward.14 = (bf16[32,5120]{1,0:T(8,128)(2,1)}, bf16[4,32,5120]{2,1,0:T(8,128)(2,1)}, bf16[4,32,5120]{2,1,0:T(8,128)(2,1)}, bf16[4,32,5120]{2,1,0:T(8,128)(2,1)...) custom-call(s32[5]{0:T(128)} %stack.31.meta, ...), custom_call_target="tpu_custom_call", output_to_operand_aliasing={{1}: (7, {}), {2}: (8, {}), {3}: (9, {}), {4}: (10, {}), {5... | custom-call | flops 469762048 | bytes 16777216 | tf_op jit(solution)/shard_map/forward/pallas_call | solution.py:483
  166.1 4.0 collective-permute-start.3
  170.2 4.8 collective-permute-done.3.inc
  184.5 1.0 backward.11
  189.3 1.0 backward.12
  194.2 1.0 backward.13
  198.3 1.0 backward.14
  200.7 1.0 backward.15
  203.1 1.0 backward.16
  205.5 1.0 backward.17
  206.4 1.3 collective-permute-start.16
  207.7 200.7 %collective-permute-done.16.inc = bf16[32,5120]{1,0:T(8,128)(2,1)S(1)} collective-permute-done((bf16[32,5120]{1,0:T(8,128)(2,1)}, bf16[32,5120]{1,0:T(8,128)(2,1)S(1)}, u32[]{:S(2)}, u32[]{:S(2)}) %collective-permute-start.16) | collective-permute-done | bytes 327712 | tf_op jit(solution)/shard_map/ppermute | solution.py:446
  409.1 8.8 %backward.18 = (bf16[32,5120]{1,0:T(8,128)(2,1)}, bf16[4,32,5120]{2,1,0:T(8,128)(2,1)}, bf16[4,32,5120]{2,1,0:T(8,128)(2,1)}, bf16[4,32,5120]{2,1,0:T(8,128)(2,1)}, bf16[2,112,4,32,128]{4,3,2,1,0:T(8,128)(2,1)}) custom-call(s32[5]{0:T(128)} %stack.31.meta, ...), custom_call_target="tpu_custom_call", output_to_operand_aliasing={{1}: (9, {}), {2}: (10, {}), {3}: (11, {}), {4}: (12, {})} | custom-call | flops 469762048 | bytes 16777216 | tf_op jit(solution)/shard_map/backward/pallas_call | solution.py:507
  417.9 1.3 collective-permute-start.17
  419.2 21.3 %collective-permute-done.17.inc = bf16[32,5120]{1,0:T(8,128)(2,1)S(1)} collective-permute-done((bf16[32,5120]{1,0:T(8,128)(2,1)}, bf16[32,5120]{1,0:T(8,128)(2,1)S(1)}, u32[]{:S(2)}, u32[]{:S(2)}) %collective-permute-start.17) | collective-permute-done | bytes 327712 | tf_op jit(solution)/shard_map/ppermute | solution.py:446
  441.2 8.8 %backward.19 = (bf16[32,5120]{1,0:T(8,128)(2,1)}, bf16[4,32,5120]{2,1,0:T(8,128)(2,1)}, bf16[4,32,5120]{2,1,0:T(8,128)(2,1)}, bf16[4,32,5120]{2,1,0:T(8,128)(2,1)}, bf16[2,112,4,32,128]{4,3,2,1,0:T(8,128)(2,1)}) custom-call(s32[5]{0:T(128)} %stack.31.meta, ...), custom_call_target="tpu_custom_call", output_to_operand_aliasing={{1}: (9, {}), {2}: (10, {}), {3}: (11, {}), {4}: (12, {})} | custom-call | flops 469762048 | bytes 16777216 | tf_op jit(solution)/shard_map/backward/pallas_call | solution.py:507
  450.1 1.3 collective-permute-start.18
  451.4 13.7 %collective-permute-done.18.inc = bf16[32,5120]{1,0:T(8,128)(2,1)S(1)} collective-permute-done((bf16[32,5120]{1,0:T(8,128)(2,1)}, bf16[32,5120]{1,0:T(8,128)(2,1)S(1)}, u32[]{:S(2)}, u32[]{:S(2)}) %collective-permute-start.18) | collective-permute-done | bytes 327712 | tf_op jit(solution)/shard_map/ppermute | solution.py:446
  465.8 8.8 %backward.20 = (bf16[32,5120]{1,0:T(8,128)(2,1)}, bf16[4,32,5120]{2,1,0:T(8,128)(2,1)}, bf16[4,32,5120]{2,1,0:T(8,128)(2,1)}, bf16[4,32,5120]{2,1,0:T(8,128)(2,1)}, bf16[2,112,4,32,128]{4,3,2,1,0:T(8,128)(2,1)}) custom-call(s32[5]{0:T(128)} %stack.31.meta, ...), custom_call_target="tpu_custom_call", output_to_operand_aliasing={{1}: (9, {}), {2}: (10, {}), {3}: (11, {}), {4}: (12, {})} | custom-call | flops 469762048 | bytes 16777216 | tf_op jit(solution)/shard_map/backward/pallas_call | solution.py:507
  474.6 1.3 collective-permute-start.19
  475.9 11.8 %collective-permute-done.19.inc = bf16[32,5120]{1,0:T(8,128)(2,1)S(1)} collective-permute-done((bf16[32,5120]{1,0:T(8,128)(2,1)}, bf16[32,5120]{1,0:T(8,128)(2,1)S(1)}, u32[]{:S(2)}, u32[]{:S(2)}) %collective-permute-start.19) | collective-permute-done | bytes 327712 | tf_op jit(solution)/shard_map/ppermute | solution.py:446
  488.4 8.8 %backward.21 = (bf16[32,5120]{1,0:T(8,128)(2,1)}, bf16[4,32,5120]{2,1,0:T(8,128)(2,1)}, bf16[4,32,5120]{2,1,0:T(8,128)(2,1)}, bf16[4,32,5120]{2,1,0:T(8,128)(2,1)}, bf16[2,112,4,32,128]{4,3,2,1,0:T(8,128)(2,1)}) custom-call(s32[5]{0:T(128)} %stack.31.meta, ...), custom_call_target="tpu_custom_call", output_to_operand_aliasing={{1}: (9, {}), {2}: (10, {}), {3}: (11, {}), {4}: (12, {})} | custom-call | flops 469762048 | bytes 16777216 | tf_op jit(solution)/shard_map/backward/pallas_call | solution.py:507
  497.3 11.7 %grads.2 = (bf16[4,4,112,8,128]{4,3,2,1,0:T(8,128)(2,1)}, bf16[4,4,112,8,128]{4,3,2,1,0:T(8,128)(2,1)}) custom-call(s32[5]{0:T(128)} %stack.31.meta, s32[2,112]{1,0:T(2,128)} %ups.47, s32[2,112]{1,0:T(2,128)} %downs.47, bf16[128,5120]{1,0:T(8,128)(2,1)} %bitcast.51, bf16[128,5120]{1,0:T(8,128)(2,1)} %bitcast.54, bf16[2,112,128,128]{3,2,1,0:T(8,128)(2,1)} %bitcast.47, ...), custom_call_target="tpu_custom_call" | custom-call | tf_op jit(solution)/shard_map/grads/pallas_call | solution.py:361
  509.0 14.0 %collective-permute-start.20 = (bf16[4,4,112,8,128]{4,3,2,1,0:T(8,128)(2,1)}, bf16[4,4,112,8,128]{4,3,2,1,0:T(8,128)(2,1)S(1)}, u32[]{:S(2)}, u32[]{:S(2)}) collective-permute-start(bf16[4,4,112,8,128]{4,3,2,1,0:T(8,128)(2,1)} %get-tuple-element.268), channel_id=1, source_target_pairs={{0,1},{1,0},{2,3},{3,2},{4,5},{5,4},{6,7},{7,6},{8,9},{9,8},{10,11... | collective-permute-start | bytes 11010056 | tf_op jit(solution)/shard_map/ppermute | solution.py:380
  523.0 9.7 %grads.3 = (bf16[4,4,112,8,128]{4,3,2,1,0:T(8,128)(2,1)}, bf16[4,4,112,8,128]{4,3,2,1,0:T(8,128)(2,1)}) custom-call(s32[5]{0:T(128)} %stack.31.meta, s32[2,112]{1,0:T(2,128)} %ups.47, s32[2,112]{1,0:T(2,128)} %downs.47, bf16[128,5120]{1,0:T(8,128)(2,1)} %bitcast.52, bf16[128,5120]{1,0:T(8,128)(2,1)} %bitcast.53, bf16[2,112,128,128]{3,2,1,0:T(8,128)(2,1)} %bitcast.48, ...), custom_call_target="tpu_custom_call" | custom-call | tf_op jit(solution)/shard_map/grads/pallas_call | solution.py:361
  533.7 1.1 concatenate.88
  534.8 1.2 collective-permute-start.21
  536.1 1.0 pad_maximum_fusion
  537.2 2.1 collective-permute-start.25
  540.3 1.1 concatenate.92
  542.5 2.2 collective-permute-start.34
  544.8 11.8 %collective-permute-done.21 = bf16[2,4,56,8,128]{4,3,2,1,0:T(8,128)(2,1)} collective-permute-done((bf16[2,4,56,8,128]{4,3,2,1,0:T(8,128)(2,1)}, bf16[2,4,56,8,128]{4,3,2,1,0:T(8,128)(2,1)}, u32[]{:S(2)}, u32[]{:S(2)}) %collective-permute-start.21) | collective-permute-done | bytes 917536 | tf_op jit(solution)/shard_map/ppermute | solution.py:380
  556.5 1.4 add_convert_fusion.5
  558.0 2.5 collective-permute-start.22
  560.5 1.7 add_convert_fusion.4
  563.0 1.4 add_convert_fusion.3
  564.4 2.7 collective-permute-start.31
  567.2 1.7 add_convert_fusion.2
  569.0 1.0 collective-permute-done.22
  571.1 1.7 collective-permute-done.26
  572.9 1.8 collective-permute-start.27
  574.7 1.5 collective-permute-done.31
  576.4 2.4 collective-permute-start.32
  578.8 1.0 collective-permute-done.35
  580.0 1.4 collective-permute-start.36
  581.4 3.3 collective-permute-done.23
  586.0 2.3 collective-permute-start.33
  588.4 1.6 collective-permute-done.24
  590.1 2.1 collective-permute-done.33
  592.6 5.2 collective-permute-start.38
  597.8 1.1 collective-permute-done.38
  598.9 1.0 broadcast_select_fusion
  (139 shorter events, 38.4 us)
Async XLA Ops:
  7.2 80.9 %all-gather.2.cloned.1.call-start = ((), (), s32[]{:S(2)}) async-start(), calls=%async_computation | async-start | bytes 15138816 | tf_op jit(solution)/shard_map/all_gather | solution.py:468
  111.0 8.7 %collective-permute-start = (bf16[32,5120]{1,0:T(8,128)(2,1)}, bf16[32,5120]{1,0:T(8,128)(2,1)S(1)}, u32[]{:S(2)}, u32[]{:S(2)}) collective-permute-start(bf16[32,5120]{1,0:T(8,128)(2,1)} %get-tuple-element.144), channel_id=1, source_target_pairs={{0,32},{1,33},{2,34},{3,35},{4,36},{5,37},{6,38},{7,39},{8,40},{9,... | collective-permute-start | bytes 983048 | tf_op jit(solution)/shard_map/ppermute | solution.py:446
  119.7 0.7 copy-start.11
  128.5 10.5 %collective-permute-start.1 = (bf16[32,5120]{1,0:T(8,128)(2,1)}, bf16[32,5120]{1,0:T(8,128)(2,1)S(1)}, u32[]{:S(2)}, u32[]{:S(2)}) collective-permute-start(bf16[32,5120]{1,0:T(8,128)(2,1)} %get-tuple-element.150), channel_id=1, source_target_pairs={{0,32},{32,64},{1,33},{33,65},{2,34},{34,66},{3,35},{35,67},{4,36}... | collective-permute-start | bytes 983048 | tf_op jit(solution)/shard_map/ppermute | solution.py:446
  139.0 0.7 copy-start.12
  147.7 9.7 %collective-permute-start.2 = (bf16[32,5120]{1,0:T(8,128)(2,1)}, bf16[32,5120]{1,0:T(8,128)(2,1)S(1)}, u32[]{:S(2)}, u32[]{:S(2)}) collective-permute-start(bf16[32,5120]{1,0:T(8,128)(2,1)} %get-tuple-element.156), channel_id=1, source_target_pairs={{0,32},{32,64},{64,96},{1,33},{33,65},{65,97},{2,34},{34,66},{66,9... | collective-permute-start | bytes 983048 | tf_op jit(solution)/shard_map/ppermute | solution.py:446
  157.4 0.7 copy-start.13
  166.1 8.8 %collective-permute-start.3 = (bf16[32,5120]{1,0:T(8,128)(2,1)}, bf16[32,5120]{1,0:T(8,128)(2,1)S(1)}, u32[]{:S(2)}, u32[]{:S(2)}) collective-permute-start(bf16[32,5120]{1,0:T(8,128)(2,1)} %get-tuple-element.162), channel_id=1, source_target_pairs={{0,32},{32,64},{64,96},{96,128},{1,33},{33,65},{65,97},{97,129},{2... | collective-permute-start | bytes 983048 | tf_op jit(solution)/shard_map/ppermute | solution.py:446
  175.0 0.7 copy-start.14
  176.6 0.7 collective-permute-start.4
  177.3 0.7 copy-start.15
  179.0 0.7 collective-permute-start.5
  179.7 0.7 copy-start.16
  181.4 0.7 collective-permute-start.6
  182.1 0.7 copy-start.10
  183.8 2.4 collective-permute-start.7
  185.5 3.1 collective-permute-start.9
  186.2 0.7 copy-start.9
  187.9 3.1 collective-permute-start.8
  188.6 0.7 copy-start.4
  190.3 3.2 collective-permute-start.11
  191.0 0.7 copy-start.5
  192.6 3.3 collective-permute-start.10
  193.5 0.7 copy-start.6
  195.2 2.4 collective-permute-start.12
  195.9 0.7 copy-start.7
  197.6 0.7 copy-start.8
  199.3 0.7 collective-permute-start.13
  200.0 0.7 copy-start.18
  201.7 0.7 collective-permute-start.14
  202.4 0.7 copy-start.19
  204.0 0.7 collective-permute-start.15
  204.7 0.7 copy-start.20
  206.4 202.0 %collective-permute-start.16 = (bf16[32,5120]{1,0:T(8,128)(2,1)}, bf16[32,5120]{1,0:T(8,128)(2,1)S(1)}, u32[]{:S(2)}, u32[]{:S(2)}) collective-permute-start(bf16[32,5120]{1,0:T(8,128)(2,1)} %get-tuple-element.243), channel_id=1, source_target_pairs={{32,0},{64,32},{96,64},{128,96},{33,1},{65,33},{97,65},{129,97},{3... | collective-permute-start | bytes 983048 | tf_op jit(solution)/shard_map/ppermute | solution.py:446
  408.4 0.7 copy-start.21
  417.9 22.6 %collective-permute-start.17 = (bf16[32,5120]{1,0:T(8,128)(2,1)}, bf16[32,5120]{1,0:T(8,128)(2,1)S(1)}, u32[]{:S(2)}, u32[]{:S(2)}) collective-permute-start(bf16[32,5120]{1,0:T(8,128)(2,1)} %get-tuple-element.248), channel_id=1, source_target_pairs={{32,0},{64,32},{96,64},{33,1},{65,33},{97,65},{34,2},{66,34},{98,6... | collective-permute-start | bytes 983048 | tf_op jit(solution)/shard_map/ppermute | solution.py:446
  440.5 0.7 copy-start.22
  450.1 15.0 %collective-permute-start.18 = (bf16[32,5120]{1,0:T(8,128)(2,1)}, bf16[32,5120]{1,0:T(8,128)(2,1)S(1)}, u32[]{:S(2)}, u32[]{:S(2)}) collective-permute-start(bf16[32,5120]{1,0:T(8,128)(2,1)} %get-tuple-element.253), channel_id=1, source_target_pairs={{32,0},{64,32},{33,1},{65,33},{34,2},{66,34},{35,3},{67,35},{36,4}... | collective-permute-start | bytes 983048 | tf_op jit(solution)/shard_map/ppermute | solution.py:446
  465.1 0.7 copy-start.23
  474.6 13.1 %collective-permute-start.19 = (bf16[32,5120]{1,0:T(8,128)(2,1)}, bf16[32,5120]{1,0:T(8,128)(2,1)S(1)}, u32[]{:S(2)}, u32[]{:S(2)}) collective-permute-start(bf16[32,5120]{1,0:T(8,128)(2,1)} %get-tuple-element.258), channel_id=1, source_target_pairs={{32,0},{33,1},{34,2},{35,3},{36,4},{37,5},{38,6},{39,7},{40,8},{41... | collective-permute-start | bytes 983048 | tf_op jit(solution)/shard_map/ppermute | solution.py:446
  487.7 0.7 copy-start.17
  509.0 23.8 %collective-permute-start.20 = (bf16[4,4,112,8,128]{4,3,2,1,0:T(8,128)(2,1)}, bf16[4,4,112,8,128]{4,3,2,1,0:T(8,128)(2,1)S(1)}, u32[]{:S(2)}, u32[]{:S(2)}) collective-permute-start(bf16[4,4,112,8,128]{4,3,2,1,0:T(8,128)(2,1)} %get-tuple-element.268), channel_id=1, source_target_pairs={{0,1},{1,0},{2,3},{3,2},{4,5},{5,4},{6,7},{7,6},{8,9},{9,8},{10,11... | collective-permute-start | bytes 11010056 | tf_op jit(solution)/shard_map/ppermute | solution.py:380
  523.0 9.8 %copy-start.3 = (bf16[4,4,112,8,128]{4,3,2,1,0:T(8,128)(2,1)S(1)}, bf16[4,4,112,8,128]{4,3,2,1,0:T(8,128)(2,1)}, u32[]{:S(2)}) copy-start(bf16[4,4,112,8,128]{4,3,2,1,0:T(8,128)(2,1)} %get-tuple-element.267) | copy-start | bytes 11010052
  532.7 6.6 %collective-permute-start.29 = (bf16[4,4,112,8,128]{4,3,2,1,0:T(8,128)(2,1)}, bf16[4,4,112,8,128]{4,3,2,1,0:T(8,128)(2,1)S(1)}, u32[]{:S(2)}, u32[]{:S(2)}) collective-permute-start(bf16[4,4,112,8,128]{4,3,2,1,0:T(8,128)(2,1)} %get-tuple-element.271), channel_id=1, source_target_pairs={{0,1},{1,0},{2,3},{3,2},{4,5},{5,4},{6,7},{7,6},{8,9},{9,8},{10,11... | collective-permute-start | bytes 11010056 | tf_op jit(solution)/shard_map/ppermute | solution.py:380
  533.7 2.4 copy-start.1
  534.8 21.7 %collective-permute-start.21 = (bf16[2,4,56,8,128]{4,3,2,1,0:T(8,128)(2,1)}, bf16[2,4,56,8,128]{4,3,2,1,0:T(8,128)(2,1)}, u32[]{:S(2)}, u32[]{:S(2)}) collective-permute-start(bf16[2,4,56,8,128]{4,3,2,1,0:T(8,128)(2,1)} %concatenate.88), channel_id=1, source_target_pairs={{0,8},{1,9},{2,10},{3,11},{4,12},{5,13},{6,14},{7,15},{8,0},{9,1},... | collective-permute-start | bytes 2752520 | tf_op jit(solution)/shard_map/ppermute | solution.py:380
  536.0 3.3 copy-start.2
  537.2 23.3 %collective-permute-start.25 = (bf16[2,4,56,8,128]{4,3,2,1,0:T(8,128)(2,1)}, bf16[2,4,56,8,128]{4,3,2,1,0:T(8,128)(2,1)}, u32[]{:S(2)}, u32[]{:S(2)}) collective-permute-start(bf16[2,4,56,8,128]{4,3,2,1,0:T(8,128)(2,1)} %pad_maximum_fusion), channel_id=1, source_target_pairs={{0,24},{1,25},{2,26},{3,27},{4,28},{5,29},{6,30},{7,31},{8,16},{9,... | collective-permute-start | bytes 2752520 | tf_op jit(solution)/shard_map/ppermute | solution.py:380
  540.3 2.1 copy-start
  541.4 21.6 %collective-permute-start.30 = (bf16[4,2,56,8,128]{4,3,2,1,0:T(8,128)(2,1)}, bf16[4,2,56,8,128]{4,3,2,1,0:T(8,128)(2,1)}, u32[]{:S(2)}, u32[]{:S(2)}) collective-permute-start(bf16[4,2,56,8,128]{4,3,2,1,0:T(8,128)(2,1)} %concatenate.92), channel_id=1, source_target_pairs={{0,2},{1,3},{2,0},{3,1},{4,6},{5,7},{6,4},{7,5},{8,10},{9,11},{10,... | collective-permute-start | bytes 2752520 | tf_op jit(solution)/shard_map/ppermute | solution.py:380
  542.5 24.6 %collective-permute-start.34 = (bf16[4,2,56,8,128]{4,3,2,1,0:T(8,128)(2,1)S(1)}, bf16[4,2,56,8,128]{4,3,2,1,0:T(8,128)(2,1)}, u32[]{:S(2)}, u32[]{:S(2)}) collective-permute-start(bf16[4,2,56,8,128]{4,3,2,1,0:T(8,128)(2,1)S(1)} %pad_maximum_fusion.1), channel_id=1, source_target_pairs={{0,6},{1,7},{2,4},{3,5},{4,2},{5,3},{6,0},{7,1},{8,14},{9,15},{10,... | collective-permute-start | bytes 2752520 | tf_op jit(solution)/shard_map/ppermute | solution.py:380
  558.0 12.0 %collective-permute-start.22 = (bf16[1,4,56,8,128]{4,3,2,1,0:T(8,128)(2,1)S(1)}, bf16[1,4,56,8,128]{4,3,2,1,0:T(8,128)(2,1)S(1)}, u32[]{:S(2)}, u32[]{:S(2)}) collective-permute-start(bf16[1,4,56,8,128]{4,3,2,1,0:T(8,128)(2,1)S(1)} %slice.183), channel_id=1, source_target_pairs={{0,24},{1,25},{2,26},{3,27},{4,28},{5,29},{6,30},{7,31},{8,16},{9,... | collective-permute-start | bytes 1376264 | tf_op jit(solution)/shard_map/ppermute | solution.py:380
  562.2 10.5 %collective-permute-start.26 = (bf16[1,4,56,8,128]{4,3,2,1,0:T(8,128)(2,1)S(1)}, bf16[1,4,56,8,128]{4,3,2,1,0:T(8,128)(2,1)S(1)}, u32[]{:S(2)}, u32[]{:S(2)}) collective-permute-start(bf16[1,4,56,8,128]{4,3,2,1,0:T(8,128)(2,1)S(1)} %slice.191), channel_id=1, source_target_pairs={{0,8},{1,9},{2,10},{3,11},{4,12},{5,13},{6,14},{7,15},{8,0},{9,1},... | collective-permute-start | bytes 1376264 | tf_op jit(solution)/shard_map/ppermute | solution.py:380
  564.4 11.9 %collective-permute-start.31 = (bf16[4,1,56,8,128]{4,3,2,1,0:T(8,128)(2,1)S(1)}, bf16[4,1,56,8,128]{4,3,2,1,0:T(8,128)(2,1)S(1)}, u32[]{:S(2)}, u32[]{:S(2)}) collective-permute-start(bf16[4,1,56,8,128]{4,3,2,1,0:T(8,128)(2,1)S(1)} %slice.199), channel_id=1, source_target_pairs={{0,6},{1,7},{2,4},{3,5},{4,2},{5,3},{6,0},{7,1},{8,14},{9,15},{10,... | collective-permute-start | bytes 1376264 | tf_op jit(solution)/shard_map/ppermute | solution.py:380
  568.9 10.9 %collective-permute-start.35 = (bf16[4,1,56,8,128]{4,3,2,1,0:T(8,128)(2,1)S(1)}, bf16[4,1,56,8,128]{4,3,2,1,0:T(8,128)(2,1)S(1)}, u32[]{:S(2)}, u32[]{:S(2)}) collective-permute-start(bf16[4,1,56,8,128]{4,3,2,1,0:T(8,128)(2,1)S(1)} %slice.207), channel_id=1, source_target_pairs={{0,2},{1,3},{2,0},{3,1},{4,6},{5,7},{6,4},{7,5},{8,10},{9,11},{10,... | collective-permute-start | bytes 1376264 | tf_op jit(solution)/shard_map/ppermute | solution.py:380
  570.2 14.5 %collective-permute-start.23 = (bf16[1,2,56,8,128]{4,3,2,1,0:T(8,128)(2,1)S(1)}, bf16[1,2,56,8,128]{4,3,2,1,0:T(8,128)(2,1)S(1)}, u32[]{:S(2)}, u32[]{:S(2)}) collective-permute-start(bf16[1,2,56,8,128]{4,3,2,1,0:T(8,128)(2,1)S(1)} %concatenate.89), channel_id=1, source_target_pairs={{0,2},{1,3},{2,0},{3,1},{4,6},{5,7},{6,4},{7,5},{8,10},{9,11},{10,... | collective-permute-start | bytes 688136 | tf_op jit(solution)/shard_map/ppermute | solution.py:380
  572.9 12.7 %collective-permute-start.27 = (bf16[1,2,56,8,128]{4,3,2,1,0:T(8,128)(2,1)S(1)}, bf16[1,2,56,8,128]{4,3,2,1,0:T(8,128)(2,1)S(1)}, u32[]{:S(2)}, u32[]{:S(2)}) collective-permute-start(bf16[1,2,56,8,128]{4,3,2,1,0:T(8,128)(2,1)S(1)} %pad_maximum_fusion.4), channel_id=1, source_target_pairs={{0,6},{1,7},{2,4},{3,5},{4,2},{5,3},{6,0},{7,1},{8,14},{9,15},{10,... | collective-permute-start | bytes 688136 | tf_op jit(solution)/shard_map/ppermute | solution.py:380
  576.4 9.4 %collective-permute-start.32 = (bf16[2,1,56,8,128]{4,3,2,1,0:T(8,128)(2,1)S(1)}, bf16[2,1,56,8,128]{4,3,2,1,0:T(8,128)(2,1)S(1)}, u32[]{:S(2)}, u32[]{:S(2)}) collective-permute-start(bf16[2,1,56,8,128]{4,3,2,1,0:T(8,128)(2,1)S(1)} %concatenate.93), channel_id=1, source_target_pairs={{0,8},{1,9},{2,10},{3,11},{4,12},{5,13},{6,14},{7,15},{8,0},{9,1},... | collective-permute-start | bytes 688136 | tf_op jit(solution)/shard_map/ppermute | solution.py:380
  580.0 8.2 %collective-permute-start.36 = (bf16[2,1,56,8,128]{4,3,2,1,0:T(8,128)(2,1)S(1)}, bf16[2,1,56,8,128]{4,3,2,1,0:T(8,128)(2,1)S(1)}, u32[]{:S(2)}, u32[]{:S(2)}) collective-permute-start(bf16[2,1,56,8,128]{4,3,2,1,0:T(8,128)(2,1)S(1)} %pad_maximum_fusion.5), channel_id=1, source_target_pairs={{0,24},{1,25},{2,26},{3,27},{4,28},{5,29},{6,30},{7,31},{8,16},{9,... | collective-permute-start | bytes 688136 | tf_op jit(solution)/shard_map/ppermute | solution.py:380
  584.8 5.2 collective-permute-start.24
  585.8 4.3 collective-permute-start.28
  586.0 6.3 %collective-permute-start.33 = (bf16[1,1,56,8,128]{4,3,2,1,0:T(8,128)(2,1)S(1)}, bf16[1,1,56,8,128]{4,3,2,1,0:T(8,128)(2,1)S(1)}, u32[]{:S(2)}, u32[]{:S(2)}) collective-permute-start(bf16[1,1,56,8,128]{4,3,2,1,0:T(8,128)(2,1)S(1)} %slice.203), channel_id=1, source_target_pairs={{0,24},{1,25},{2,26},{3,27},{4,28},{5,29},{6,30},{7,31},{8,16},{9,... | collective-permute-start | bytes 344072 | tf_op jit(solution)/shard_map/ppermute | solution.py:380
  588.3 4.0 collective-permute-start.37
  592.6 6.3 %collective-permute-start.38 = (bf16[2,112,4,128]{3,2,1,0:T(4,128)(2,1)S(1)}, bf16[2,112,4,128]{3,2,1,0:T(4,128)(2,1)S(1)}, u32[]{:S(2)}, u32[]{:S(2)}) collective-permute-start(bf16[2,112,4,128]{3,2,1,0:T(4,128)(2,1)S(1)} %broadcast_select_fusion.2), channel_id=1, source_target_pairs={{0,1},{1,0},{2,3},{3,2},{4,5},{5,4},{6,7},{7,6},{8,9},{9,8},{10,11... | collective-permute-start | bytes 688136 | tf_op jit(solution)/shard_map/ppermute | solution.py:380
Sparse Core Ops, SparseCore 0:
  11.1 76.9 all-gather.1
